TPU v7x, 32 devices: a whole 2x2x4 slice. The times are simulated.
32 devices in a mesh: row: 4 (over x, core), col: 8 (over z, y).
Axes of the slice: x: 2, y: 2, z: 4, core: 2. Of those that a mesh axis runs over, the one named last changes fastest.
Arguments:
- vectors: bfloat16 [32, 8192], P(None, ('row', 'col')), may hold values from -6 to 6
- tiles: bfloat16 [512, 256, 256], P(('row', 'col')), may hold values from -0.09375 to 0.09375
- tile_rows: int32 [512], P(('row', 'col')), may hold values from 0 to 7, as said below
- tile_cols: int32 [512], P(('row', 'col')), may hold values from 0 to 3, as said below
- tile_live: int32 [32], P(('row', 'col')), may hold values from 2 to 16, as said below
Outputs:
- first: bfloat16 [32, 8192], P(None, ('row', 'col'))
- second: bfloat16 [32, 8192], P(None, ('row', 'col'))
Inputs may be any that keep to these rules, and one draw needn't show every extreme that they name: `tile_rows`: A slot's row block is counted among the 8 row blocks of its device's row index, and its global row block never exceeds its global column block. `tile_cols`: A slot's column block is counted among the 4 column blocks of its device's column index. Each device uses its first tile_live slots; some device uses all 16.
All inputs are finite; a program needn't handle non-finite values.
Results may differ from a plain program's by a relative error of at most 0.0044.
Values may be sent and summed in bfloat16 or wider, within the bound.
No kernel may reach another device: no remote copies, remote signals or barrier semaphores. Data moves between devices by JAX's collectives and lax.ppermute only.
A program may use at most 64 MiB of HBM per device.

v0:
```python
import jax
import jax.numpy as jnp
from jax import lax
from jax.sharding import PartitionSpec as P


def half_direct(colset, tiles, rows, keep, count_rows):
    width = colset.shape[0]
    size = tiles.shape[1]
    picked = jnp.take(colset.reshape(width, -1, size), rows[1], axis=1)
    direct = jnp.einsum("ktj,tij->kti", picked, tiles, preferred_element_type=jnp.float32)
    row_hot = (rows[0][:, None] == jnp.arange(count_rows, dtype=jnp.int32)[None, :]).astype(
        jnp.float32
    ) * keep[:, None]
    placed = jnp.einsum("kti,ta->kai", direct, row_hot, precision=lax.Precision.HIGHEST)
    return placed.reshape(width, count_rows * size)


def half_mirror(rowset, tiles, cols, keep, count_cols):
    width = rowset.shape[0]
    size = tiles.shape[1]
    picked = jnp.take(rowset.reshape(width, -1, size), cols[1], axis=1)
    mirror = jnp.einsum("kti,tij->ktj", picked, tiles, preferred_element_type=jnp.float32)
    col_hot = (cols[0][:, None] == jnp.arange(count_cols, dtype=jnp.int32)[None, :]).astype(
        jnp.float32
    ) * keep[:, None]
    placed = jnp.einsum("ktj,tb->kbj", mirror, col_hot, precision=lax.Precision.HIGHEST)
    return placed.reshape(width, count_cols * size)


def sum_rows(direct):
    return lax.psum_scatter(direct, "col", scatter_dimension=1, tiled=True)


def sum_cols(mirror):
    return lax.psum_scatter(mirror, "row", scatter_dimension=1, tiled=True)


def gather_rowset(vec):
    return lax.all_gather(vec, "col", axis=1, tiled=True)


def both_halves(vec, rowset, tiles, tile_rows, tile_cols, tile_live):
    size = tiles.shape[1]
    count = tiles.shape[0]
    keep = (jnp.arange(count, dtype=jnp.int32) < tile_live[0]).astype(jnp.float32)
    colset = lax.all_gather(vec, "row", axis=1, tiled=True)
    count_rows = rowset.shape[1] // size
    count_cols = colset.shape[1] // size
    direct = half_direct(colset, tiles, (tile_rows, tile_cols), keep, count_rows)
    mirror = half_mirror(rowset, tiles, (tile_cols, tile_rows), keep, count_cols)
    return (direct, sum_cols(mirror))


def local(vectors, tiles, tile_rows, tile_cols, tile_live):
    direct, own_cols = both_halves(
        vectors, gather_rowset(vectors), tiles, tile_rows, tile_cols, tile_live
    )
    first = (sum_rows(direct) + own_cols).astype(jnp.bfloat16)
    next_rowset = gather_rowset(first)
    direct_two, cols_two = both_halves(first, next_rowset, tiles, tile_rows, tile_cols, tile_live)
    second_f = 2.0 * (sum_rows(direct_two) + cols_two) - vectors.astype(jnp.float32)
    return (first, second_f.astype(jnp.bfloat16))


def solution(mesh):
    placed = (
        P(None, ("row", "col")),
        P(("row", "col"), None, None),
        P(("row", "col")),
        P(("row", "col")),
        P(("row", "col")),
    )
    return jax.shard_map(
        local,
        mesh=mesh,
        in_specs=placed,
        out_specs=(P(None, ("row", "col")), P(None, ("row", "col"))),
        check_vma=False,
    )
```

profile of v0, /device:TPU:0, one launch (start us, length us, event | category | flops | bytes accessed | tf_op | source)
XLA Modules:
  0.0 261.5 jit_solution(1111360292076652762)
XLA Ops:
  7.2 0.8 compare_select_fusion
  8.0 0.7 compare_and_fusion
  9.4 32.5 %all_gather.13 = bf16[32,2048]{1,0:T(8,128)(2,1)S(1)} all-gather(bf16[32,256]{1,0:T(8,128)(2,1)} %param.9), channel_id=1, replica_groups=mesh['row'=4,'col'=8] {'col'}, dimensions={1}, use_global_device_ids=true | all-gather | bytes 147456 | tf_op jit(solution)/shard_map/all_gather | solution.py:40
  41.9 0.6 gather_fusion.1
  43.0 0.6 fusion.4
  43.7 0.7 copy.20
  44.4 5.2 %all_gather.12 = bf16[32,1024]{1,0:T(8,128)(2,1)S(1)} all-gather(bf16[32,256]{1,0:T(8,128)(2,1)S(1)} %copy-done.2), channel_id=1, replica_groups=mesh['row'=4,'col'=8] {'row'}, dimensions={1}, use_global_device_ids=true | all-gather | bytes 81920 | tf_op jit(solution)/shard_map/all_gather | solution.py:47
  49.7 0.6 gather_fusion
  50.3 0.7 convolution_bitcast_fusion.3
  51.0 0.7 fusion.6
  51.7 0.8 copy.19
  52.5 12.5 %reduce-scatter.7.cloned.1.call-done = f32[32,256]{1,0:T(8,128)} async-done(((f32[32,1024]{1,0:T(8,128)}), f32[32,256]{1,0:T(8,128)}) %reduce-scatter.7.cloned.1.call-update) | async-done | bytes 32784 | tf_op jit(solution)/shard_map/reduce_scatter | solution.py:36
  65.0 65.4 %reduce-scatter.5.cloned.1.call-done = f32[32,256]{1,0:T(8,128)} async-done(((f32[32,2048]{1,0:T(8,128)}), f32[32,256]{1,0:T(8,128)}) %reduce-scatter.5.cloned.1.call-update) | async-done | bytes 32784 | tf_op jit(solution)/shard_map/reduce_scatter | solution.py:32
  130.4 0.8 add_convert_fusion
  131.2 5.2 %all_gather.14 = bf16[32,1024]{1,0:T(8,128)(2,1)S(1)} all-gather(bf16[32,256]{1,0:T(8,128)(2,1)S(1)} %add_convert_fusion), channel_id=1, replica_groups=mesh['row'=4,'col'=8] {'row'}, dimensions={1}, use_global_device_ids=true | all-gather | bytes 81920 | tf_op jit(solution)/shard_map/all_gather | solution.py:47
  136.4 30.5 %all_gather.15 = bf16[32,2048]{1,0:T(8,128)(2,1)S(1)} all-gather(bf16[32,256]{1,0:T(8,128)(2,1)S(1)} %add_convert_fusion), channel_id=1, replica_groups=mesh['row'=4,'col'=8] {'col'}, dimensions={1}, use_global_device_ids=true | all-gather | bytes 147456 | tf_op jit(solution)/shard_map/all_gather | solution.py:40
  168.6 0.6 fusion
  169.3 0.7 copy.22
  170.0 0.7 convolution_bitcast_fusion.1
  170.7 0.7 fusion.2
  171.4 0.8 copy.21
  172.2 16.5 %reduce-scatter.11.cloned.1.call-done = f32[32,256]{1,0:T(8,128)} async-done(((f32[32,1024]{1,0:T(8,128)}), f32[32,256]{1,0:T(8,128)}) %reduce-scatter.11.cloned.1.call-update) | async-done | bytes 32784 | tf_op jit(solution)/shard_map/reduce_scatter | solution.py:36
  188.7 64.9 %reduce-scatter.9.cloned.1.call-done = f32[32,256]{1,0:T(8,128)} async-done(((f32[32,2048]{1,0:T(8,128)}), f32[32,256]{1,0:T(8,128)}) %reduce-scatter.9.cloned.1.call-update) | async-done | bytes 32784 | tf_op jit(solution)/shard_map/reduce_scatter | solution.py:32
  253.6 1.4 subtract_convert_fusion
  (31 shorter events, 2.5 us)
Async XLA Ops:
  7.2 35.3 %copy-start = (bf16[16,256,256]{2,1,0:T(8,128)(2,1)S(1)}, bf16[16,256,256]{2,1,0:T(8,128)(2,1)}, u32[]{:S(2)}) copy-start(bf16[16,256,256]{2,1,0:T(8,128)(2,1)} %param.10) | copy-start | bytes 6291460
  7.2 35.8 %copy-start.3 = (s32[16]{0:T(128)S(1)}, s32[16]{0:T(128)}, u32[]{:S(2)}) copy-start(s32[16]{0:T(128)} %param.12) | copy-start | bytes 196
  7.2 57.8 %reduce-scatter.7.cloned.1.call-start = ((), (), s32[]{:S(2)}) async-start(), calls=%async_computation.5 | async-start | bytes 163840 | tf_op jit(solution)/shard_map/reduce_scatter | solution.py:36
  42.5 1.9 copy-start.2
  43.7 7.4 %copy-start.4 = (s32[16]{0:T(128)S(1)}, s32[16]{0:T(128)}, u32[]{:S(2)}) copy-start(s32[16]{0:T(128)} %param.11) | copy-start | bytes 196
  44.4 86.0 %reduce-scatter.5.cloned.1.call-start = ((), (), s32[]{:S(2)}) async-start(), calls=%async_computation.4 | async-start | bytes 294912 | tf_op jit(solution)/shard_map/reduce_scatter | solution.py:32
  52.5 136.2 %reduce-scatter.11.cloned.1.call-start = ((), (), s32[]{:S(2)}) async-start(), calls=%async_computation.7 | async-start | bytes 163840 | tf_op jit(solution)/shard_map/reduce_scatter | solution.py:36
  131.2 37.4 %copy-start.1 = (bf16[32,256]{1,0:T(8,128)(2,1)}, bf16[32,256]{1,0:T(8,128)(2,1)S(1)}, u32[]{:S(2)}) copy-start(bf16[32,256]{1,0:T(8,128)(2,1)S(1)} %add_convert_fusion) | copy-start | bytes 49156
  170.0 83.6 %reduce-scatter.9.cloned.1.call-start = ((), (), s32[]{:S(2)}) async-start(), calls=%async_computation.6 | async-start | bytes 294912 | tf_op jit(solution)/shard_map/reduce_scatter | solution.py:32
Sparse Core Ops, SparseCore 0:
  44.5 20.4 reduce-scatter.6
  68.7 61.6 reduce-scatter.4
  170.1 18.5 reduce-scatter.10
  191.9 61.6 reduce-scatter.8
where the time goes:
time: 262 us
  waiting for transfers between devices  159 us (61%)
  blocking collectives  73.5 us (28%)
  between operations  14.6 us (6%)
  local copies, waits for them, and re-layouts  5.23 us (2%)
  matrix products  5.03 us (2%)
  other arithmetic  3.65 us (1%)
    reduce_scatter x2, waiting for transfers between devices, sum_rows(): return lax.psum_scatter(direct, 'col', scatter_dimension=1, tiled=True)  130 us
    all_gather x2, blocking collectives, gather_rowset(): return lax.all_gather(vec, 'col', axis=1, tiled=True)  63 us
    reduce_scatter x2, waiting for transfers between devices, sum_cols(): return lax.psum_scatter(mirror, 'row', scatter_dimension=1, tiled=True)  29 us
    all_gather x2, blocking collectives, both_halves(): colset = lax.all_gather(vec, 'row', axis=1, tiled=True)  10.5 us
  transfers between devices with their start and end apart: 4, of which 4 were waited for; matrix products, arithmetic and copies ran while one was open for 2% of the time, Pallas kernels for 0%

commit v1 on v0

--- a/solution.py
+++ b/solution.py
@@ -44,7 +44,12 @@
     size = tiles.shape[1]
     count = tiles.shape[0]
     keep = (jnp.arange(count, dtype=jnp.int32) < tile_live[0]).astype(jnp.float32)
-    colset = lax.all_gather(vec, "row", axis=1, tiled=True)
+    ring = [vec]
+    for hop in range(3):
+        ring.append(lax.ppermute(ring[-1], "row", [(dev, (dev + 1) % 4) for dev in range(4)]))
+    colset = jnp.roll(
+        jnp.concatenate(ring[::-1], axis=1), (lax.axis_index("row") + 1) * ring[0].shape[1], axis=1
+    )
     count_rows = rowset.shape[1] // size
     count_cols = colset.shape[1] // size
     direct = half_direct(colset, tiles, (tile_rows, tile_cols), keep, count_rows)

time: 262 us -> 259 us (0.989)
  blocking collectives: 73.5 us -> 62.9 us
  waiting for transfers between devices: 159 us -> 166 us
    ppermute x0 -> x6, waiting for transfers between devices: none -> 10.7 us  [both_halves(): lax.ppermute(ring[-1], 'row', [(dev, (dev + 1) % 4) for dev in range(4)])]
    all_gather x2 -> x0, blocking collectives: 10.5 us -> none  [both_halves(): colset = lax.all_gather(vec, 'row', axis=1, tiled=True)]
    reduce_scatter x2, waiting for transfers between devices: 29 us -> 25.3 us  [sum_cols(): return lax.psum_scatter(mirror, 'row', scatter_dimension=1, tiled=True)]
  transfers between devices with their start and end apart: 4 -> 10, of which waited for: 4 -> 8; matrix products, arithmetic and copies ran while one was open for 2% -> 5% of each run, Pallas kernels for 0% -> 0%
where the time goes in v1:
time: 259 us
  waiting for transfers between devices  166 us (64%)
  blocking collectives  62.9 us (24%)
  between operations  14.7 us (6%)
  local copies, waits for them, and re-layouts  5.29 us (2%)
  matrix products  5.04 us (2%)
  other arithmetic  3.93 us (2%)
    reduce_scatter x2, waiting for transfers between devices, sum_rows(): return lax.psum_scatter(direct, 'col', scatter_dimension=1, tiled=True)  130 us
    all_gather x2, blocking collectives, gather_rowset(): return lax.all_gather(vec, 'col', axis=1, tiled=True)  62.9 us
    reduce_scatter x2, waiting for transfers between devices, sum_cols(): return lax.psum_scatter(mirror, 'row', scatter_dimension=1, tiled=True)  25.3 us
    ppermute x6, waiting for transfers between devices, both_halves(): lax.ppermute(ring[-1], 'row', [(dev, (dev + 1) % 4) for dev in range(4)])  10.7 us
  transfers between devices with their start and end apart: 10, of which 8 were waited for; matrix products, arithmetic and copies ran while one was open for 5% of the time, Pallas kernels for 0%

profile of v1, /device:TPU:0, one launch (start us, length us, event | category | flops | bytes accessed | tf_op | source)
XLA Modules:
  0.0 259.0 jit_solution(14689056998107084794)
XLA Ops:
  7.7 32.2 %all_gather.6 = bf16[32,2048]{1,0:T(8,128)(2,1)S(1)} all-gather(bf16[32,256]{1,0:T(8,128)(2,1)} %param.11), channel_id=1, replica_groups=mesh['row'=4,'col'=8] {'col'}, dimensions={1}, use_global_device_ids=true | all-gather | bytes 147456 | tf_op jit(solution)/shard_map/all_gather | solution.py:40
  40.0 0.7 compare_select_fusion
  40.6 0.7 compare_and_fusion
  43.1 0.7 fusion.4
  43.8 0.7 copy.20
  44.6 3.1 %collective-permute-done.1 = bf16[32,256]{1,0:T(8,128)(2,1)S(1)} collective-permute-done((bf16[32,256]{1,0:T(8,128)(2,1)S(1)}, bf16[32,256]{1,0:T(8,128)(2,1)S(1)}, u32[]{:S(2)}, u32[]{:S(2)}) %collective-permute-start.1) | collective-permute-done | bytes 16416 | tf_op jit(solution)/shard_map/ppermute | solution.py:49
  47.8 3.1 %collective-permute-done.2 = bf16[32,256]{1,0:T(8,128)(2,1)S(1)} collective-permute-done((bf16[32,256]{1,0:T(8,128)(2,1)S(1)}, bf16[32,256]{1,0:T(8,128)(2,1)S(1)}, u32[]{:S(2)}, u32[]{:S(2)}) %collective-permute-start.2) | collective-permute-done | bytes 16416 | tf_op jit(solution)/shard_map/ppermute | solution.py:49
  51.7 0.7 convolution_bitcast_fusion.3
  52.5 0.7 fusion.6
  53.1 0.8 copy.19
  54.0 11.1 %reduce-scatter.7.cloned.1.call-done = f32[32,256]{1,0:T(8,128)} async-done(((f32[32,1024]{1,0:T(8,128)}), f32[32,256]{1,0:T(8,128)}) %reduce-scatter.7.cloned.1.call-update) | async-done | bytes 32784 | tf_op jit(solution)/shard_map/reduce_scatter | solution.py:36
  65.1 65.4 %reduce-scatter.5.cloned.1.call-done = f32[32,256]{1,0:T(8,128)} async-done(((f32[32,2048]{1,0:T(8,128)}), f32[32,256]{1,0:T(8,128)}) %reduce-scatter.5.cloned.1.call-update) | async-done | bytes 32784 | tf_op jit(solution)/shard_map/reduce_scatter | solution.py:32
  130.5 0.8 add_convert_fusion
  131.3 30.7 %all_gather.7 = bf16[32,2048]{1,0:T(8,128)(2,1)S(1)} all-gather(bf16[32,256]{1,0:T(8,128)(2,1)S(1)} %add_convert_fusion), channel_id=1, replica_groups=mesh['row'=4,'col'=8] {'col'}, dimensions={1}, use_global_device_ids=true | all-gather | bytes 147456 | tf_op jit(solution)/shard_map/all_gather | solution.py:40
  163.2 2.7 %collective-permute-done.4 = bf16[32,256]{1,0:T(8,128)(2,1)S(1)} collective-permute-done((bf16[32,256]{1,0:T(8,128)(2,1)S(1)}, bf16[32,256]{1,0:T(8,128)(2,1)S(1)}, u32[]{:S(2)}, u32[]{:S(2)}) %collective-permute-start.4) | collective-permute-done | bytes 16416 | tf_op jit(solution)/shard_map/ppermute | solution.py:49
  165.8 0.7 fusion
  166.5 0.7 copy.22
  167.3 1.7 collective-permute-done.5
  169.8 0.7 convolution_bitcast_fusion.1
  170.5 0.7 fusion.2
  171.2 0.8 copy.21
  172.0 14.1 %reduce-scatter.11.cloned.1.call-done = f32[32,256]{1,0:T(8,128)} async-done(((f32[32,1024]{1,0:T(8,128)}), f32[32,256]{1,0:T(8,128)}) %reduce-scatter.11.cloned.1.call-update) | async-done | bytes 32784 | tf_op jit(solution)/shard_map/reduce_scatter | solution.py:36
  186.1 64.9 %reduce-scatter.9.cloned.1.call-done = f32[32,256]{1,0:T(8,128)} async-done(((f32[32,2048]{1,0:T(8,128)}), f32[32,256]{1,0:T(8,128)}) %reduce-scatter.9.cloned.1.call-update) | async-done | bytes 32784 | tf_op jit(solution)/shard_map/reduce_scatter | solution.py:32
  251.1 1.4 subtract_convert_fusion
  (42 shorter events, 4.7 us)
Async XLA Ops:
  7.2 35.4 %copy-start = (bf16[16,256,256]{2,1,0:T(8,128)(2,1)S(1)}, bf16[16,256,256]{2,1,0:T(8,128)(2,1)}, u32[]{:S(2)}) copy-start(bf16[16,256,256]{2,1,0:T(8,128)(2,1)} %param.12) | copy-start | bytes 6291460
  7.2 35.9 %copy-start.3 = (s32[16]{0:T(128)S(1)}, s32[16]{0:T(128)}, u32[]{:S(2)}) copy-start(s32[16]{0:T(128)} %param.14) | copy-start | bytes 196
  7.2 57.9 %reduce-scatter.7.cloned.1.call-start = ((), (), s32[]{:S(2)}) async-start(), calls=%async_computation.5 | async-start | bytes 163840 | tf_op jit(solution)/shard_map/reduce_scatter | solution.py:36
  7.2 37.3 %collective-permute-start = (bf16[32,256]{1,0:T(8,128)(2,1)}, bf16[32,256]{1,0:T(8,128)(2,1)S(1)}, u32[]{:S(2)}, u32[]{:S(2)}) collective-permute-start(bf16[32,256]{1,0:T(8,128)(2,1)} %param.11), channel_id=1, source_target_pairs={{0,8},{8,16},{16,24},{24,0},{1,9},{9,17},{17,25},{25,1},{2,10},{10... | collective-permute-start | bytes 49160 | tf_op jit(solution)/shard_map/ppermute | solution.py:49
  42.6 8.4 %copy-start.2 = (bf16[32,256]{1,0:T(8,128)(2,1)S(1)}, bf16[32,256]{1,0:T(8,128)(2,1)}, u32[]{:S(2)}) copy-start(bf16[32,256]{1,0:T(8,128)(2,1)} %param.11) | copy-start | bytes 49156
  43.7 8.7 %copy-start.4 = (s32[16]{0:T(128)S(1)}, s32[16]{0:T(128)}, u32[]{:S(2)}) copy-start(s32[16]{0:T(128)} %param.13) | copy-start | bytes 196
  44.5 86.0 %reduce-scatter.5.cloned.1.call-start = ((), (), s32[]{:S(2)}) async-start(), calls=%async_computation.4 | async-start | bytes 294912 | tf_op jit(solution)/shard_map/reduce_scatter | solution.py:32
  44.5 3.2 %collective-permute-start.1 = (bf16[32,256]{1,0:T(8,128)(2,1)S(1)}, bf16[32,256]{1,0:T(8,128)(2,1)S(1)}, u32[]{:S(2)}, u32[]{:S(2)}) collective-permute-start(bf16[32,256]{1,0:T(8,128)(2,1)S(1)} %collective-permute-done), channel_id=1, source_target_pairs={{0,8},{8,16},{16,24},{24,0},{1,9},{9,17},{17,25},{25,1},{2,10},{10... | collective-permute-start | bytes 49160 | tf_op jit(solution)/shard_map/ppermute | solution.py:49
  47.7 3.2 %collective-permute-start.2 = (bf16[32,256]{1,0:T(8,128)(2,1)S(1)}, bf16[32,256]{1,0:T(8,128)(2,1)S(1)}, u32[]{:S(2)}, u32[]{:S(2)}) collective-permute-start(bf16[32,256]{1,0:T(8,128)(2,1)S(1)} %collective-permute-done.1), channel_id=1, source_target_pairs={{0,8},{8,16},{16,24},{24,0},{1,9},{9,17},{17,25},{25,1},{2,10},{10... | collective-permute-start | bytes 49160 | tf_op jit(solution)/shard_map/ppermute | solution.py:49
  53.9 132.2 %reduce-scatter.11.cloned.1.call-start = ((), (), s32[]{:S(2)}) async-start(), calls=%async_computation.7 | async-start | bytes 163840 | tf_op jit(solution)/shard_map/reduce_scatter | solution.py:36
  131.3 37.7 %copy-start.1 = (bf16[32,256]{1,0:T(8,128)(2,1)}, bf16[32,256]{1,0:T(8,128)(2,1)S(1)}, u32[]{:S(2)}) copy-start(bf16[32,256]{1,0:T(8,128)(2,1)S(1)} %add_convert_fusion) | copy-start | bytes 49156
  131.3 31.3 %collective-permute-start.3 = (bf16[32,256]{1,0:T(8,128)(2,1)S(1)}, bf16[32,256]{1,0:T(8,128)(2,1)S(1)}, u32[]{:S(2)}, u32[]{:S(2)}) collective-permute-start(bf16[32,256]{1,0:T(8,128)(2,1)S(1)} %add_convert_fusion), channel_id=1, source_target_pairs={{0,8},{8,16},{16,24},{24,0},{1,9},{9,17},{17,25},{25,1},{2,10},{10... | collective-permute-start | bytes 49160 | tf_op jit(solution)/shard_map/ppermute | solution.py:49
  162.6 3.2 %collective-permute-start.4 = (bf16[32,256]{1,0:T(8,128)(2,1)S(1)}, bf16[32,256]{1,0:T(8,128)(2,1)S(1)}, u32[]{:S(2)}, u32[]{:S(2)}) collective-permute-start(bf16[32,256]{1,0:T(8,128)(2,1)S(1)} %collective-permute-done.3), channel_id=1, source_target_pairs={{0,8},{8,16},{16,24},{24,0},{1,9},{9,17},{17,25},{25,1},{2,10},{10... | collective-permute-start | bytes 49160 | tf_op jit(solution)/shard_map/ppermute | solution.py:49
  165.8 3.2 %collective-permute-start.5 = (bf16[32,256]{1,0:T(8,128)(2,1)S(1)}, bf16[32,256]{1,0:T(8,128)(2,1)S(1)}, u32[]{:S(2)}, u32[]{:S(2)}) collective-permute-start(bf16[32,256]{1,0:T(8,128)(2,1)S(1)} %collective-permute-done.4), channel_id=1, source_target_pairs={{0,8},{8,16},{16,24},{24,0},{1,9},{9,17},{17,25},{25,1},{2,10},{10... | collective-permute-start | bytes 49160 | tf_op jit(solution)/shard_map/ppermute | solution.py:49
  167.2 83.9 %reduce-scatter.9.cloned.1.call-start = ((), (), s32[]{:S(2)}) async-start(), calls=%async_computation.6 | async-start | bytes 294912 | tf_op jit(solution)/shard_map/reduce_scatter | solution.py:32
Sparse Core Ops, SparseCore 0:
  44.6 20.4 reduce-scatter.6
  68.8 61.6 reduce-scatter.4
  167.3 18.7 reduce-scatter.10
  189.3 61.6 reduce-scatter.8
